TPU v7x, 256 devices: a whole 4x4x8 slice. The times are simulated.
256 devices in a mesh: nodes: 8 (over x, core), batch: 32 (over z, y).
Axes of the slice: x: 4, y: 4, z: 8, core: 2. Of those that a mesh axis runs over, the one named last changes fastest.
Arguments:
- leaves: float32 [16, 128, 4096], P('nodes', None, 'batch'), may hold values from -340 to 8
- prod_child: int32 [16, 2], replicated, may hold values from 0 to 15
- block_weight: float32 [1024, 128, 128], P('nodes'), may hold values from 0.0001 to 0.01
- block_child: int32 [8, 128], P('nodes'), may hold values from 0 to 15
- block_parent: int32 [8, 128], P('nodes'), may hold values from 0 to 3, as said below
- block_count: int32 [8], P('nodes'), may hold values from 32 to 128, as said below
- upper_flow: float32 [32, 128, 4096], P('nodes', None, 'batch'), may hold values from 0.1 to 1
Outputs:
- sum_values: float32 [32, 128, 4096], P('nodes', None, 'batch')
- leaf_flow: float32 [16, 128, 4096], P('nodes', None, 'batch')
- param_flow: float32 [1024, 128, 128], P(('nodes', 'batch'))
Inputs may be any that keep to these rules, and one draw needn't show every extreme that they name: `block_parent`: every owner's first 4 slots name its sum groups 0 to 3 in order. `block_count`: some owner has all 128 slots live.
All inputs are finite; a program needn't handle non-finite values.
Results may differ from a plain program's by a relative error of at most 0.0003.
Values sent between devices are 32-bit elements; how exact they have to be, the bound alone decides.
No kernel may reach another device: no remote copies, remote signals or barrier semaphores. Data moves between devices by JAX's collectives and lax.ppermute only.
A program may use at most 128 MiB of HBM per device.

v0:
```python
import jax
import jax.numpy as jnp
from jax import lax
from jax.sharding import PartitionSpec as P

very_low = -1e30
high = lax.Precision.HIGHEST


def body(leaves, prod_child, block_weight, block_child, block_parent, block_count, upper_flow):
    group_leaf = leaves.shape[0]
    owners = lax.axis_size("nodes")
    total_leaf = group_leaf * owners
    total_prod = prod_child.shape[0]
    prod_each = total_prod // owners
    sum_each = upper_flow.shape[0]
    blocks = block_weight.shape[0]
    mine = lax.axis_index("nodes")
    first = jax.nn.one_hot(prod_child[:, 0], total_leaf, dtype=jnp.float32)
    second = jax.nn.one_hot(prod_child[:, 1], total_leaf, dtype=jnp.float32)
    select = first + second
    own_select = lax.dynamic_slice_in_dim(select, mine * prod_each, prod_each, 0)
    columns = own_select
    own_prod = jnp.einsum(
        "pg,gjs->pjs",
        columns,
        lax.all_gather(leaves, "nodes", axis=0, tiled=True),
        precision=high,
        preferred_element_type=jnp.float32,
    )
    products = lax.all_gather(own_prod, "nodes", axis=0, tiled=True)
    peak = jnp.max(products, axis=1)
    child = block_child.reshape(-1)
    parent = block_parent.reshape(-1)
    live = jnp.arange(blocks, dtype=jnp.int32) < block_count[0]
    parent_hot = jax.nn.one_hot(parent, sum_each, dtype=jnp.float32) * live[:, None].astype(
        jnp.float32
    )
    child_peak = jnp.where(live[:, None], peak[child], very_low)
    top = jnp.max(jnp.where(parent_hot[:, :, None] > 0.0, child_peak[:, None, :], very_low), axis=0)
    diff = products[child] - top[parent][:, None, :]
    shifted = jnp.exp(jnp.where(live[:, None, None], diff, very_low))
    mixed = jnp.einsum(
        "bij,bjs->bis", block_weight, shifted, precision=high, preferred_element_type=jnp.float32
    )
    total = jnp.einsum(
        "bq,bis->qis", parent_hot, mixed, precision=high, preferred_element_type=jnp.float32
    )
    sum_values = top[:, None, :] + jnp.log(total)
    factor = upper_flow / total
    parent_factor = factor[parent]
    back = jnp.einsum(
        "bij,bis->bjs",
        block_weight,
        parent_factor,
        precision=high,
        preferred_element_type=jnp.float32,
    )
    child_term = shifted * back
    child_hot = jax.nn.one_hot(child, total_prod, dtype=jnp.float32) * live[:, None].astype(
        jnp.float32
    )
    columns = child_hot
    product_flow = lax.psum_scatter(
        jnp.einsum(
            "bc,bjs->cjs", columns, child_term, precision=high, preferred_element_type=jnp.float32
        ),
        "nodes",
        scatter_dimension=0,
        tiled=True,
    )
    columns = own_select
    leaf_flow = lax.psum_scatter(
        jnp.einsum(
            "pg,pjs->gjs", columns, product_flow, precision=high, preferred_element_type=jnp.float32
        ),
        "nodes",
        scatter_dimension=0,
        tiled=True,
    )
    param_flow = lax.psum_scatter(
        block_weight
        * jnp.einsum(
            "bis,bjs->bij",
            parent_factor,
            shifted,
            precision=high,
            preferred_element_type=jnp.float32,
        ),
        "batch",
        scatter_dimension=0,
        tiled=True,
    )
    return (sum_values, leaf_flow, param_flow)


def solution(mesh):
    placed = (
        P("nodes", None, "batch"),
        P(),
        P("nodes", None, None),
        P("nodes", None),
        P("nodes", None),
        P("nodes"),
        P("nodes", None, "batch"),
    )
    return jax.shard_map(
        body,
        mesh=mesh,
        in_specs=placed,
        out_specs=(
            P("nodes", None, "batch"),
            P("nodes", None, "batch"),
            P(("nodes", "batch"), None, None),
        ),
        check_vma=False,
    )
```

profile of v0, /device:TPU:2, one launch (start us, length us, event | category | flops | bytes accessed | tf_op | source)
XLA Modules:
  0.0 481.1 jit_solution(5586205592342857914)
XLA Ops:
  7.2 0.7 all-gather.3.cloned.1.call-update
  7.9 0.8 slice_bitcast_fusion.1
  8.9 28.1 %all-gather.3.cloned.1.call-done = f32[16,128,128]{2,1,0:T(8,128)} async-done(((f32[2,128,128]{2,1,0:T(8,128)}), f32[16,128,128]{2,1,0:T(8,128)}) %all-gather.3.cloned.1.call-update) | async-done | bytes 1048592 | tf_op jit(solution)/shard_map/all_gather | solution.py:27
  37.0 2.4 fusion.10
  39.4 0.7 copy.52
  40.8 0.7 fusion.28
  41.5 0.7 fusion.29
  42.1 0.7 select_compare_fusion
  42.8 23.1 %all-gather.5.cloned.1.call-done = f32[16,128,128]{2,1,0:T(8,128)} async-done(((f32[2,128,128]{2,1,0:T(8,128)}), f32[16,128,128]{2,1,0:T(8,128)}) %all-gather.5.cloned.1.call-update) | async-done | bytes 1048592 | tf_op jit(solution)/shard_map/all_gather | solution.py:31
  65.9 1.3 reduce_max.18
  67.2 0.6 gather_fusion
  67.8 5.5 %gather_fusion.1 = f32[128,128,128]{2,1,0:T(8,128)} fusion(f32[16,128,128]{2,1,0:T(8,128)} %all-gather.5.cloned.1.call-done, s32[1024]{0:T(1024)S(1)} %pad_clamp_fusion.1), kind=kCustom, calls=%fused_computation.1 | custom fusion | bytes 16777728 | tf_op jit(solution)/shard_map/gather | solution.py:41
  73.4 9.0 %copy.53 = f32[128,128,128]{1,2,0:T(8,128)} copy(f32[128,128,128]{2,1,0:T(8,128)} %gather_fusion.1) | data formatting | bytes 16777216 | tf_op jit(solution)/shard_map/gather | solution.py:41
  82.4 0.1 broadcast_select_fusion
  82.5 0.1 select_reduce_fusion
  82.6 0.6 gather_fusion.2
  83.3 23.7 %fusion.8 = f32[128,128,128]{1,2,0:T(8,128)} fusion(f32[128,128,128]{2,1,0:T(8,128)} %param.9, f32[128,128,128]{1,2,0:T(8,128)} %copy.53, f32[128,128]{1,0:T(8,128)S(1)} %gather_fusion.2, pred[128]{0:T(512)(128)(4,1)S(1)} %get-tuple-element.22), kind=kOutput, calls=%fused_computation.14 | convolution fusion | flops 3225419776 | bytes 25231488 | tf_op jit(solution)/shard_map/bij,bjs->bis/dot_general | solution.py:43
  107.0 9.3 %copy.54 = f32[128,128,128]{2,0,1:T(8,128)} copy(f32[128,128,128]{1,2,0:T(8,128)} %fusion.8) | data formatting | bytes 16777216 | tf_op jit(solution)/shard_map/bij,bjs->bis/dot_general | solution.py:43
  116.3 6.4 %log_add_fusion = (f32[4,128,128]{2,0,1:T(4,128)S(1)}, f32[4,128,128]{2,0,1:T(4,128)S(1)}) fusion(f32[4,128]{1,0:T(4,128)S(1)} %select_reduce_fusion, f32[128,128,128]{2,0,1:T(8,128)} %copy.54, f32[128]{0:T(128)S(1)} %get-tuple-element.23, s32[128]{0:T(128)S(1)} %bitcast.40), kind=kOutput, calls=%fused_computation.19 | convolution fusion | flops 100729856 | bytes 8915968 | tf_op jit(solution)/shard_map/bq,bis->qis/dot_general | solution.py:46
  122.8 4.3 gather_fusion.3
  127.1 22.4 %bitcast_multiply_fusion = f32[128,128,128]{1,2,0:T(8,128)} fusion(f32[128,128,128]{1,2,0:T(8,128)} %copy.53, f32[128,128]{1,0:T(8,128)S(1)} %gather_fusion.2, pred[128]{0:T(512)(128)(4,1)S(1)} %get-tuple-element.22, f32[128,128,128]{2,1,0:T(8,128)} %gather_fusion.3, f32[128,128,128]{2,1,0:T(8,128)} %param.9), kind=kOutput, calls=%fused_computation.4 | convolution fusion | flops 3227516928 | bytes 33620096 | tf_op jit(solution)/shard_map/bij,bis->bjs/dot_general | solution.py:52
  149.5 9.3 %copy.57 = f32[128,128,128]{2,0,1:T(8,128)} copy(f32[128,128,128]{1,2,0:T(8,128)} %bitcast_multiply_fusion) | data formatting | bytes 16777216 | tf_op jit(solution)/shard_map/mul | solution.py:59
  158.7 6.4 %fusion.14 = f32[16,128,128]{2,0,1:T(8,128)S(1)} fusion(f32[128,128,128]{2,0,1:T(8,128)} %copy.57, f32[128]{0:T(128)S(1)} %get-tuple-element.23, s32[128]{0:T(128)S(1)} %bitcast.38), kind=kOutput, calls=%fused_computation.24 | convolution fusion | flops 402657280 | bytes 9438208 | tf_op jit(solution)/shard_map/bc,bjs->cjs/dot_general | solution.py:65
  165.1 1.3 copy.58
  166.5 0.3 reduce-scatter.6.cloned.1.call-start
  166.7 33.1 %reduce-scatter.4.cloned.1.call-done = f32[2,128,128]{2,1,0:T(8,128)} async-done(((f32[16,128,128]{2,1,0:T(8,128)}), f32[2,128,128]{2,1,0:T(8,128)}) %reduce-scatter.4.cloned.1.call-update) | async-done | bytes 131088 | tf_op jit(solution)/shard_map/reduce_scatter | solution.py:64
  199.8 2.0 fusion.12
  201.9 1.4 copy.60
  203.3 16.9 %fusion.9 = f32[128,128,128]{2,1,0:T(8,128)} fusion(f32[128,128,128]{2,1,0:T(8,128)} %param.9, f32[128,128,128]{2,1,0:T(8,128)} %gather_fusion.3, f32[128,128,128]{1,2,0:T(8,128)} %copy.53, f32[128,128]{1,0:T(8,128)S(1)} %gather_fusion.2, pred[128]{0:T(512)(128)(4,1)S(1)} %get-tuple-element.22), kind=kOutput, calls=%fused_computation.15 | convolution fusion | flops 3227516928 | bytes 33620096 | tf_op jit(solution)/shard_map/bis,bjs->bij/dot_general | solution.py:83
  220.3 0.7 copy.62
  221.0 16.1 %reduce-scatter.6.cloned.1.call-done = f32[2,128,128]{2,1,0:T(8,128)} async-done(((f32[16,128,128]{2,1,0:T(8,128)}), f32[2,128,128]{2,1,0:T(8,128)}) %reduce-scatter.6.cloned.1.call-update) | async-done | bytes 131088 | tf_op jit(solution)/shard_map/reduce_scatter | solution.py:73
  237.1 237.5 %reduce-scatter.8.cloned.1.call-done = f32[4,128,128]{2,1,0:T(8,128)} async-done(((f32[128,128,128]{2,1,0:T(8,128)}), f32[4,128,128]{2,1,0:T(8,128)}) %reduce-scatter.8.cloned.1.call-update) | async-done | bytes 262160 | tf_op jit(solution)/shard_map/reduce_scatter | solution.py:81
  (20 shorter events, 0.4 us)
Async XLA Ops:
  7.2 29.8 %all-gather.3.cloned.1.call-start = ((), (), s32[]{:S(2)}) async-start(), calls=%async_computation.3 | async-start | bytes 1179648 | tf_op jit(solution)/shard_map/all_gather | solution.py:27
  7.9 58.0 %all-gather.5.cloned.1.call-start = ((), (), s32[]{:S(2)}) async-start(), calls=%async_computation.4 | async-start | bytes 1179648 | tf_op jit(solution)/shard_map/all_gather | solution.py:31
  40.1 159.7 %reduce-scatter.4.cloned.1.call-start = ((), (), s32[]{:S(2)}) async-start(), calls=%async_computation.5 | async-start | bytes 1179648 | tf_op jit(solution)/shard_map/reduce_scatter | solution.py:64
  107.0 9.3 %copy-start.2 = (s32[1,128]{1,0:T(1,128)S(1)}, s32[1,128]{1,0:T(1,128)}, u32[]{:S(2)}) copy-start(s32[1,128]{1,0:T(1,128)} %param.11) | copy-start | bytes 1540
  116.3 6.4 %copy-start = (f32[4,128,128]{2,1,0:T(8,128)S(1)}, f32[4,128,128]{2,1,0:T(8,128)}, u32[]{:S(2)}) copy-start(f32[4,128,128]{2,1,0:T(8,128)} %param.13) | copy-start | bytes 786436
  149.5 9.3 %copy-start.1 = (s32[1,128]{1,0:T(1,128)S(1)}, s32[1,128]{1,0:T(1,128)}, u32[]{:S(2)}) copy-start(s32[1,128]{1,0:T(1,128)} %param.10) | copy-start | bytes 1540
  166.5 70.6 %reduce-scatter.6.cloned.1.call-start = ((), (), s32[]{:S(2)}) async-start(), calls=%async_computation.6 | async-start | bytes 1179648 | tf_op jit(solution)/shard_map/reduce_scatter | solution.py:73
  203.3 271.3 %reduce-scatter.8.cloned.1.call-start = ((), (), s32[]{:S(2)}) async-start(), calls=%async_computation.7 | async-start | bytes 8650752 | tf_op jit(solution)/shard_map/reduce_scatter | solution.py:81
Sparse Core Ops, SparseCore 0:
  9.8 27.1 all-gather.2
  40.2 25.6 all-gather.4
  166.6 33.1 reduce-scatter.3
  203.4 33.6 reduce-scatter.5
  241.5 232.9 reduce-scatter.7
where the time goes:
time: 482 us; the launch traced here: 481 us
  waiting for transfers between devices  339 us (70%)
  matrix products  80.3 us (17%)
  local copies, waits for them, and re-layouts  43.7 us (9%)
  between operations  14.5 us (3%)
    reduce_scatter x1, waiting for transfers between devices, body(): lax.psum_scatter(block_weight * jnp.einsum('bis,bjs->bij', parent_factor,...  237 us
    reduce_scatter x1, waiting for transfers between devices, body(): lax.psum_scatter(jnp.einsum('bc,bjs->cjs', columns, child_term, precision...  33.1 us
    all_gather x1, waiting for transfers between devices, body(): lax.all_gather(leaves, 'nodes', axis=0, tiled=True)  28.1 us
    dot_general x1, matrix products, body(): jnp.einsum('bij,bjs->bis', block_weight, shifted, precision=high, preferr...  23.7 us
    all_gather x1, waiting for transfers between devices, body(): products = lax.all_gather(own_prod, 'nodes', axis=0, tiled=True)  23.1 us
    dot_general x1, matrix products, body(): jnp.einsum('bij,bis->bjs', block_weight, parent_factor, precision=high, p...  22.4 us
    dot_general x1, matrix products, body(): jnp.einsum('bis,bjs->bij', parent_factor, shifted, precision=high, prefer...  16.9 us
    reduce_scatter x1, waiting for transfers between devices, body(): lax.psum_scatter(jnp.einsum('pg,pjs->gjs', columns, product_flow, precisi...  16.1 us
  transfers between devices with their start and end apart: 5, of which 5 were waited for; matrix products, arithmetic and copies ran while one was open for 4% of the time, Pallas kernels for 0%

commit v1 on v0

--- a/solution.py
+++ b/solution.py
@@ -5,6 +5,19 @@
 
 very_low = -1e30
 high = lax.Precision.HIGHEST
+
+
+def collect(x, axis, dim):
+    ways = lax.axis_size(axis)
+    up = [(d, (d + 1) % ways) for d in range(ways)]
+    down = [(d, (d - 1) % ways) for d in range(ways)]
+    earlier, later = ([x], [x])
+    for _ in range(ways // 2):
+        earlier.append(lax.ppermute(earlier[-1], axis, up))
+    for _ in range((ways - 1) // 2):
+        later.append(lax.ppermute(later[-1], axis, down))
+    line = jnp.concatenate([*earlier[::-1], *later[1:]], axis=dim)
+    return jnp.roll(line, (lax.axis_index(axis) - ways // 2) * x.shape[dim], axis=dim)
 
 
 def body(leaves, prod_child, block_weight, block_child, block_parent, block_count, upper_flow):
@@ -24,7 +37,7 @@
     own_prod = jnp.einsum(
         "pg,gjs->pjs",
         columns,
-        lax.all_gather(leaves, "nodes", axis=0, tiled=True),
+        collect(leaves, "nodes", 0),
         precision=high,
         preferred_element_type=jnp.float32,
     )

time: 482 us -> 473 us (0.981)
  waiting for transfers between devices: 339 us -> 324 us
  starting transfers between devices: 0.42 us -> 6.05 us
    all_gather x1 -> x0, waiting for transfers between devices: 28.1 us -> none  [body(): lax.all_gather(leaves, 'nodes', axis=0, tiled=True)]
    ppermute x0 -> x7, waiting for transfers between devices: none -> 11 us  [the longest x4 10.8 us: collect(): earlier.append(lax.ppermute(earlier[-1], axis, up))]
    ppermute x0 -> x7, starting transfers between devices: none -> 5.66 us  [the longest x3 5.64 us: collect(): later.append(lax.ppermute(later[-1], axis, down))]
  transfers between devices with their start and end apart: 5 -> 11, of which waited for: 5 -> 9; matrix products, arithmetic and copies ran while one was open for 4% -> 4% of each run, Pallas kernels for 0% -> 0%
where the time goes in v1:
time: 473 us
  waiting for transfers between devices  324 us (68%)
  matrix products  78.6 us (17%)
  local copies, waits for them, and re-layouts  46.8 us (10%)
  between operations  14.5 us (3%)
  starting transfers between devices  6.05 us (1%)
    reduce_scatter x1, waiting for transfers between devices, body(): lax.psum_scatter(block_weight * jnp.einsum('bis,bjs->bij', parent_factor,...  237 us
    reduce_scatter x1, waiting for transfers between devices, body(): lax.psum_scatter(jnp.einsum('bc,bjs->cjs', columns, child_term, precision...  33.1 us
    all_gather x1, waiting for transfers between devices, body(): products = lax.all_gather(own_prod, 'nodes', axis=0, tiled=True)  27 us
    dot_general x1, matrix products, body(): jnp.einsum('bij,bjs->bis', block_weight, shifted, precision=high, preferr...  23.7 us
    dot_general x1, matrix products, body(): jnp.einsum('bij,bis->bjs', block_weight, parent_factor, precision=high, p...  22.4 us
    dot_general x1, matrix products, body(): jnp.einsum('bis,bjs->bij', parent_factor, shifted, precision=high, prefer...  16.9 us
    reduce_scatter x1, waiting for transfers between devices, body(): lax.psum_scatter(jnp.einsum('pg,pjs->gjs', columns, product_flow, precisi...  16 us
    gather x3, local copies, waits for them, and re-layouts, body(): diff = products[child] - top[parent][:, None, :]  15.3 us
  transfers between devices with their start and end apart: 11, of which 9 were waited for; matrix products, arithmetic and copies ran while one was open for 4% of the time, Pallas kernels for 0%

profile of v1, /device:TPU:2, one launch (start us, length us, event | category | flops | bytes accessed | tf_op | source)
XLA Modules:
  0.0 472.7 jit_solution(2668815109971319671)
XLA Ops:
  7.2 1.0 copy.63
  8.2 1.7 collective-permute-start.4
  10.0 2.6 collective-permute-done
  12.6 2.0 collective-permute-start.5
  14.7 2.4 collective-permute-done.1
  17.2 1.9 collective-permute-start.6
  19.1 2.4 collective-permute-done.2
  21.4 0.8 slice_bitcast_fusion.1
  22.3 3.5 collective-permute-done.3
  25.8 1.9 concatenate.6
  27.7 0.7 fusion.10
  28.4 0.7 copy.67
  29.8 0.7 fusion.28
  31.1 0.7 select_compare_fusion
  31.8 27.0 %all-gather.2.cloned.1.call-done = f32[16,128,128]{2,1,0:T(8,128)} async-done(((f32[2,128,128]{2,1,0:T(8,128)}), f32[16,128,128]{2,1,0:T(8,128)}) %all-gather.2.cloned.1.call-update) | async-done | bytes 1048592 | tf_op jit(solution)/shard_map/all_gather | solution.py:44
  58.8 5.5 %gather_fusion.1 = f32[128,128,128]{2,1,0:T(8,128)} fusion(f32[16,128,128]{2,1,0:T(8,128)} %all-gather.2.cloned.1.call-done, s32[1024]{0:T(1024)S(1)} %pad_clamp_fusion.1), kind=kCustom, calls=%fused_computation.1 | custom fusion | bytes 16777728 | tf_op jit(solution)/shard_map/gather | solution.py:54
  64.3 9.1 %copy.68 = f32[128,128,128]{1,2,0:T(8,128)} copy(f32[128,128,128]{2,1,0:T(8,128)} %gather_fusion.1) | data formatting | bytes 16777216 | tf_op jit(solution)/shard_map/gather | solution.py:54
  75.0 23.7 %fusion.8 = f32[128,128,128]{1,2,0:T(8,128)} fusion(f32[128,128,128]{2,1,0:T(8,128)} %param.9, f32[128,128,128]{1,2,0:T(8,128)} %copy.68, f32[128,128]{1,0:T(8,128)S(1)} %gather_fusion.2, pred[128]{0:T(512)(128)(4,1)S(1)} %get-tuple-element.22), kind=kOutput, calls=%fused_computation.14 | convolution fusion | flops 3225419776 | bytes 25231488 | tf_op jit(solution)/shard_map/bij,bjs->bis/dot_general | solution.py:56
  98.8 9.3 %copy.69 = f32[128,128,128]{2,0,1:T(8,128)} copy(f32[128,128,128]{1,2,0:T(8,128)} %fusion.8) | data formatting | bytes 16777216 | tf_op jit(solution)/shard_map/bij,bjs->bis/dot_general | solution.py:56
  108.0 6.4 %log_add_fusion = (f32[4,128,128]{2,0,1:T(4,128)S(1)}, f32[4,128,128]{2,0,1:T(4,128)S(1)}) fusion(f32[4,128]{1,0:T(4,128)S(1)} %select_reduce_fusion, f32[128,128,128]{2,0,1:T(8,128)} %copy.69, f32[128]{0:T(128)S(1)} %get-tuple-element.23, s32[128]{0:T(128)S(1)} %bitcast.40), kind=kOutput, calls=%fused_computation.19 | convolution fusion | flops 100729856 | bytes 8915968 | tf_op jit(solution)/shard_map/bq,bis->qis/dot_general | solution.py:59
  114.5 4.3 gather_fusion.3
  118.9 22.4 %bitcast_multiply_fusion = f32[128,128,128]{1,2,0:T(8,128)} fusion(f32[128,128,128]{1,2,0:T(8,128)} %copy.68, f32[128,128]{1,0:T(8,128)S(1)} %gather_fusion.2, pred[128]{0:T(512)(128)(4,1)S(1)} %get-tuple-element.22, f32[128,128,128]{2,1,0:T(8,128)} %gather_fusion.3, f32[128,128,128]{2,1,0:T(8,128)} %param.9), kind=kOutput, calls=%fused_computation.4 | convolution fusion | flops 3227516928 | bytes 33620096 | tf_op jit(solution)/shard_map/bij,bis->bjs/dot_general | solution.py:65
  141.2 9.3 %copy.72 = f32[128,128,128]{2,0,1:T(8,128)} copy(f32[128,128,128]{1,2,0:T(8,128)} %bitcast_multiply_fusion) | data formatting | bytes 16777216 | tf_op jit(solution)/shard_map/mul | solution.py:72
  150.6 6.4 %fusion.14 = f32[16,128,128]{2,0,1:T(8,128)S(1)} fusion(f32[128,128,128]{2,0,1:T(8,128)} %copy.72, f32[128]{0:T(128)S(1)} %get-tuple-element.23, s32[128]{0:T(128)S(1)} %bitcast.38), kind=kOutput, calls=%fused_computation.24 | convolution fusion | flops 402657280 | bytes 9438208 | tf_op jit(solution)/shard_map/bc,bjs->cjs/dot_general | solution.py:78
  156.9 1.3 copy.73
  158.5 33.1 %reduce-scatter.4.cloned.1.call-done = f32[2,128,128]{2,1,0:T(8,128)} async-done(((f32[16,128,128]{2,1,0:T(8,128)}), f32[2,128,128]{2,1,0:T(8,128)}) %reduce-scatter.4.cloned.1.call-update) | async-done | bytes 131088 | tf_op jit(solution)/shard_map/reduce_scatter | solution.py:77
  191.6 2.0 fusion.12
  193.7 1.4 copy.75
  195.1 16.9 %fusion.9 = f32[128,128,128]{2,1,0:T(8,128)} fusion(f32[128,128,128]{2,1,0:T(8,128)} %param.9, f32[128,128,128]{2,1,0:T(8,128)} %gather_fusion.3, f32[128,128,128]{1,2,0:T(8,128)} %copy.68, f32[128,128]{1,0:T(8,128)S(1)} %gather_fusion.2, pred[128]{0:T(512)(128)(4,1)S(1)} %get-tuple-element.22), kind=kOutput, calls=%fused_computation.15 | convolution fusion | flops 3227516928 | bytes 33620096 | tf_op jit(solution)/shard_map/bis,bjs->bij/dot_general | solution.py:96
  212.1 0.7 copy.77
  212.8 16.0 %reduce-scatter.6.cloned.1.call-done = f32[2,128,128]{2,1,0:T(8,128)} async-done(((f32[16,128,128]{2,1,0:T(8,128)}), f32[2,128,128]{2,1,0:T(8,128)}) %reduce-scatter.6.cloned.1.call-update) | async-done | bytes 131088 | tf_op jit(solution)/shard_map/reduce_scatter | solution.py:86
  228.8 237.4 %reduce-scatter.8.cloned.1.call-done = f32[4,128,128]{2,1,0:T(8,128)} async-done(((f32[128,128,128]{2,1,0:T(8,128)}), f32[4,128,128]{2,1,0:T(8,128)}) %reduce-scatter.8.cloned.1.call-update) | async-done | bytes 262160 | tf_op jit(solution)/shard_map/reduce_scatter | solution.py:94
  (35 shorter events, 3.1 us)
Async XLA Ops:
  7.2 51.6 %all-gather.2.cloned.1.call-start = ((), (), s32[]{:S(2)}) async-start(), calls=%async_computation.3 | async-start | bytes 1179648 | tf_op jit(solution)/shard_map/all_gather | solution.py:44
  8.2 4.4 collective-permute-start
  8.2 4.4 collective-permute-start.4
  12.6 4.4 collective-permute-start.1
  12.6 4.6 collective-permute-start.5
  17.0 4.4 collective-permute-start.2
  17.2 5.1 %collective-permute-start.6 = (f32[2,128,128]{2,0,1:T(2,128)S(1)}, f32[2,128,128]{2,0,1:T(2,128)S(1)}, u32[]{:S(2)}, u32[]{:S(2)}) collective-permute-start(f32[2,128,128]{2,0,1:T(2,128)S(1)} %collective-permute-done.5), channel_id=1, source_target_pairs={{0,224},{32,0},{64,32},{96,64},{128,96},{160,128},{192,160},{224,1... | collective-permute-start | bytes 393224 | tf_op jit(solution)/shard_map/ppermute | solution.py:18
  21.4 4.4 collective-permute-start.3
  29.1 162.5 %reduce-scatter.4.cloned.1.call-start = ((), (), s32[]{:S(2)}) async-start(), calls=%async_computation.4 | async-start | bytes 1179648 | tf_op jit(solution)/shard_map/reduce_scatter | solution.py:77
  64.3 9.1 %copy-start = (f32[16,128,128]{2,1,0:T(8,128)S(1)}, f32[16,128,128]{2,1,0:T(8,128)}, u32[]{:S(2)}) copy-start(f32[16,128,128]{2,1,0:T(8,128)} %all-gather.2.cloned.1.call-done) | copy-start | bytes 3145732
  98.8 9.3 %copy-start.3 = (s32[1,128]{1,0:T(1,128)S(1)}, s32[1,128]{1,0:T(1,128)}, u32[]{:S(2)}) copy-start(s32[1,128]{1,0:T(1,128)} %param.11) | copy-start | bytes 1540
  108.0 6.4 %copy-start.1 = (f32[4,128,128]{2,1,0:T(8,128)S(1)}, f32[4,128,128]{2,1,0:T(8,128)}, u32[]{:S(2)}) copy-start(f32[4,128,128]{2,1,0:T(8,128)} %param.13) | copy-start | bytes 786436
  141.2 9.3 %copy-start.2 = (s32[1,128]{1,0:T(1,128)S(1)}, s32[1,128]{1,0:T(1,128)}, u32[]{:S(2)}) copy-start(s32[1,128]{1,0:T(1,128)} %param.10) | copy-start | bytes 1540
  158.3 70.6 %reduce-scatter.6.cloned.1.call-start = ((), (), s32[]{:S(2)}) async-start(), calls=%async_computation.5 | async-start | bytes 1179648 | tf_op jit(solution)/shard_map/reduce_scatter | solution.py:86
  195.1 271.1 %reduce-scatter.8.cloned.1.call-start = ((), (), s32[]{:S(2)}) async-start(), calls=%async_computation.6 | async-start | bytes 8650752 | tf_op jit(solution)/shard_map/reduce_scatter | solution.py:94
Sparse Core Ops, SparseCore 0:
  29.2 29.5 all-gather.1
  158.4 33.1 reduce-scatter.3
  195.2 33.5 reduce-scatter.5
  233.3 232.8 reduce-scatter.7
